TPU v7x, 256 devices: a whole 4x4x8 slice. The times are simulated.
256 devices in a mesh: branch: 64 (over z, y, x_lo), rows: 4 (over x_hi, core).
Axes of the slice: x: 4 (x_hi: 2, x_lo: 2; x = x_hi * 2 + x_lo), y: 4, z: 8, core: 2. Of those that a mesh axis runs over, the one named last changes fastest.
Arguments:
- points: float32 [3, 524288], P(None, ('branch', 'rows')), may hold values from 0 to 1, as said below
- noise: float32 [524288], P(('branch', 'rows')), may hold values from 0.2 to 2
- landmarks: float32 [7, 3, 256], replicated, may hold values from 0 to 1, as said below
- mixing: float32 [7, 256, 256], replicated, may hold values from -6 to 6
Outputs:
- bases: float32 [3, 524288, 256], P(None, ('branch', 'rows'))
- factors: float32 [64, 3, 256, 256], P('branch')
Inputs may be any that keep to these rules, and one draw needn't show every extreme that they name: `points`: coordinates lie in the unit cube. `landmarks`: coordinates lie in the unit cube.
All inputs are finite; a program needn't handle non-finite values.
Results may differ from a plain program's by a relative error of at most 0.00025.
Values sent between devices are 32-bit elements; how exact they have to be, the bound alone decides.
A program may use at most 128 MiB of HBM per device.

v0:
```python
import jax
import jax.numpy as jnp
from jax import lax
from jax.sharding import PartitionSpec as P

highest = lax.Precision.HIGHEST


def partner(value, axis, bit):
    return lax.ppermute(value, axis, [(i, i ^ 1 << bit) for i in range(lax.axis_size(axis))])


def kernel_block(positions, landmark_set, length_scale):
    spread = jnp.zeros((positions.shape[1], landmark_set.shape[1]), jnp.float32)
    for component in range(3):
        offset = positions[component][:, None] - landmark_set[component][None, :]
        spread = spread + offset * offset
    return jnp.exp(-spread / (2.0 * length_scale * length_scale))


def project(left, right):
    return jnp.einsum(
        "nr,ns->rs", left, right, precision=highest, preferred_element_type=jnp.float32
    )


def solve_with(factor, right_side):
    return jax.scipy.linalg.cho_solve((factor, True), right_side)


def group_total(partial_value, width_bits):
    summed = lax.psum(partial_value, "rows")
    for bit_index in range(width_bits):
        summed = summed + partner(summed, "branch", bit_index)
    return summed


def on_device(points, noise, landmarks, mixing):
    width_rank = mixing.shape[1]
    local_rows = points.shape[1]
    branch_bits = lax.axis_size("branch").bit_length() - 1
    row_devices = lax.axis_size("rows")
    length_scale = 0.6 * width_rank ** (-1.0 / 3.0)
    position = lax.axis_index("branch")
    identity = jnp.eye(width_rank, dtype=jnp.float32)
    unit_list = []
    node_bits = []
    node_rows = []
    for level_index in range(3):
        width_bits = branch_bits - 2 + level_index
        node_id = 2 ** (2 - level_index) - 1 + position // 2**width_bits
        landmark_set = lax.dynamic_index_in_dim(landmarks, node_id, 0, keepdims=False)
        mixing_now = lax.dynamic_index_in_dim(mixing, node_id, 0, keepdims=False)
        kernel = kernel_block(points, landmark_set, length_scale)
        unit_list.append(
            jnp.dot(kernel, mixing_now, precision=highest, preferred_element_type=jnp.float32)
        )
        node_bits.append(width_bits)
        node_rows.append(float(2**width_bits * row_devices * local_rows))
    bases = []
    factor_list = []
    coefficients = {}
    for level_index in range(3):
        for prior_index in range(level_index):
            cross = group_total(
                project(bases[prior_index], unit_list[level_index]), node_bits[prior_index]
            )
            coefficients[prior_index, level_index] = (
                solve_with(factor_list[prior_index], cross) / node_rows[prior_index]
            )
        current = unit_list[level_index] / noise[:, None]
        for prior_index in range(level_index):
            current = current - jnp.dot(
                bases[prior_index],
                coefficients[prior_index, level_index],
                precision=highest,
                preferred_element_type=jnp.float32,
            )
        bases.append(current)
        gram_matrix = group_total(project(current, unit_list[level_index]), node_bits[level_index])
        factor = jnp.linalg.cholesky(identity + gram_matrix / node_rows[level_index])
        factor_list.append(factor)
    return (jnp.stack(bases, axis=0), jnp.stack(factor_list, axis=0)[None])


def solution(mesh):
    in_specs = (P(None, ("branch", "rows")), P(("branch", "rows")), P(), P())
    out_specs = (P(None, ("branch", "rows"), None), P("branch", None, None, None))
    return jax.shard_map(
        on_device, mesh=mesh, in_specs=in_specs, out_specs=out_specs, check_vma=False
    )
```

profile of v0, /device:TPU:8, one launch (start us, length us, event | category | flops | bytes accessed | tf_op | source)
XLA Modules:
  0.0 528.9 jit_solution(15413675945931273060)
XLA Ops:
  9.1 2.5 fusion.24
  11.6 4.7 fusion.127
  20.1 5.1 fusion.126
  25.2 50.5 %all-reduce.11.cloned.1.call-done = (f32[256,256]{0,1:T(8,128)}, f32[256,256]{1,0:T(8,128)}) async-done(((f32[256,256]{0,1:T(8,128)}, f32[256,256]{1,0:T(8,128)}), (f32[256,256]{0,1:T(8,128)}, f32[256,256]{1,0:T(8,128)})) %all-reduce.11.cloned.1.call-update) | async-done | bytes 524304 | tf_op jit(solution)/shard_map/psum | solution.py:32
  77.7 7.4 %collective-permute-done = f32[256,256]{0,1:T(8,128)S(1)} collective-permute-done((f32[256,256]{0,1:T(8,128)}, f32[256,256]{0,1:T(8,128)S(1)}, u32[]{:S(2)}, u32[]{:S(2)}) %collective-permute-start) | collective-permute-done | bytes 262176 | tf_op jit(solution)/shard_map/ppermute | solution.py:10
  86.7 3.4 collective-permute-done.4
  102.6 4.3 collective-permute-done.2
  108.6 4.6 fusion.125
  114.2 11.7 %cholesky.172 = f32[128,128]{1,0:T(8,128)S(1)} custom-call(f32[128,128]{1,0:T(8,128)S(1)} %cholesky.270), custom_call_target="Cholesky" | custom-call | tf_op jit(solution)/shard_map/jit(cholesky)/cholesky | solution.py:81
  126.0 9.8 %custom-call.17 = f32[1,128,128]{1,2,0:T(8,128)S(1)} custom-call(f32[1,128,128]{2,1,0:T(8,128)S(1)} %get-tuple-element.67), custom_call_target="InvertDiagBlocksLowerTriangular" | custom-call | tf_op jit(solution)/shard_map/jit(cholesky)/cholesky | solution.py:81
  136.3 11.7 %cholesky.189 = f32[128,128]{1,0:T(8,128)S(1)} custom-call(f32[128,128]{1,0:T(8,128)S(1)} %convolution_subtract_fusion.8), custom_call_target="Cholesky" | custom-call | tf_op jit(solution)/shard_map/jit(cholesky)/cholesky | solution.py:81
  150.1 4.0 while.6
  154.2 19.9 %custom-call.18 = f32[2,128,128]{1,2,0:T(8,128)S(1)} custom-call(f32[2,128,128]{2,1,0:T(8,128)S(1)} %get-tuple-element.24), custom_call_target="InvertDiagBlocksLowerTriangular" | custom-call | tf_op jit(solution)/shard_map/jit(_cho_solve)/triangular_solve | solution.py:28
  176.1 4.3 convolution_subtract_fusion.2
  180.5 4.3 fusion.132
  184.8 4.3 fusion.133
  189.1 47.9 %all-reduce.9.cloned.1.call-done = (f32[256,256]{1,0:T(8,128)}, f32[256,256]{1,0:T(8,128)}, f32[256,256]{0,1:T(8,128)}) async-done(((f32[256,256]{1,0:T(8,128)}, f32[256,256]{1,0:T(8,128)}, f32[256,256]{0,1:T(8,128)}), (f32[256,256]{1,0:T(8,128)}, f32[256,256]{1,0:T(8,128)}, f32[256,256]{0,1:T(8,128)})) %all-reduce.9.cloned.1.call-update) | async-done | bytes 786448 | tf_op jit(solution)/shard_map/psum | solution.py:32
  239.7 6.8 %collective-permute-done.12 = f32[256,256]{0,1:T(8,128)S(1)} collective-permute-done((f32[256,256]{0,1:T(8,128)}, f32[256,256]{0,1:T(8,128)S(1)}, u32[]{:S(2)}, u32[]{:S(2)}) %collective-permute-start.12) | collective-permute-done | bytes 262176 | tf_op jit(solution)/shard_map/ppermute | solution.py:10
  248.5 3.6 collective-permute-done.8
  253.7 3.4 collective-permute-done.17
  258.8 2.5 collective-permute-start.14
  263.4 4.0 collective-permute-done.18
  269.6 4.3 collective-permute-done.14
  275.6 3.9 collective-permute-done.10
  281.2 2.9 collective-permute-done.19
  285.8 2.6 collective-permute-start.16
  290.8 6.4 %collective-permute-done.20 = f32[256,256]{1,0:T(8,128)S(1)} collective-permute-done((f32[256,256]{1,0:T(8,128)S(1)}, f32[256,256]{1,0:T(8,128)S(1)}, u32[]{:S(2)}, u32[]{:S(2)}) %collective-permute-start.20) | collective-permute-done | bytes 262176 | tf_op jit(solution)/shard_map/ppermute | solution.py:10
  298.4 5.5 %convolution_subtract_fusion.1 = f32[2048,256]{1,0:T(8,128)} fusion(f32[2048,256]{1,0:T(8,128)} %copy-done.5, f32[2048]{0:T(1024)S(1)} %copy-done.13, f32[128,256]{0,1:T(8,128)} %copy.9, f32[128,256]{0,1:T(8,128)S(1)} %fusion.103, f32[2048,256]{1,0:T(8,128)} %copy-done.8), kind=kOutput, calls=%fused_computation.6 | convolution fusion | flops 1612316672 | bytes 6561792 | tf_op jit(solution)/shard_map/dot_general | solution.py:73
  305.1 11.7 %cholesky.206 = f32[128,128]{1,0:T(8,128)S(1)} custom-call(f32[128,128]{1,0:T(8,128)S(1)} %cholesky.273), custom_call_target="Cholesky" | custom-call | tf_op jit(solution)/shard_map/jit(cholesky)/cholesky | solution.py:81
  316.8 9.8 %custom-call.20 = f32[1,128,128]{1,2,0:T(8,128)S(1)} custom-call(f32[1,128,128]{2,1,0:T(8,128)S(1)} %get-tuple-element.63), custom_call_target="InvertDiagBlocksLowerTriangular" | custom-call | tf_op jit(solution)/shard_map/jit(cholesky)/cholesky | solution.py:81
  327.1 12.1 %cholesky.223 = f32[128,128]{1,0:T(8,128)S(1)} custom-call(f32[128,128]{1,0:T(8,128)S(1)} %convolution_subtract_fusion.7), custom_call_target="Cholesky" | custom-call | tf_op jit(solution)/shard_map/jit(cholesky)/cholesky | solution.py:81
  342.0 4.1 while.7
  346.0 19.7 %custom-call.21 = f32[2,128,128]{1,2,0:T(8,128)S(1)} custom-call(f32[2,128,128]{2,1,0:T(8,128)S(1)} %get-tuple-element.26), custom_call_target="InvertDiagBlocksLowerTriangular" | custom-call | tf_op jit(solution)/shard_map/jit(_cho_solve)/triangular_solve | solution.py:28
  367.8 4.4 convolution_subtract_fusion
  373.5 4.3 fusion.134
  377.8 45.7 %all-reduce.7.cloned.1.call-done = f32[256,256]{0,1:T(8,128)} async-done(((f32[256,256]{0,1:T(8,128)}), f32[256,256]{0,1:T(8,128)}) %all-reduce.7.cloned.1.call-update) | async-done | bytes 262160 | tf_op jit(solution)/shard_map/psum | solution.py:32
  424.1 8.2 %collective-permute-done.22 = f32[256,256]{0,1:T(8,128)S(1)} collective-permute-done((f32[256,256]{0,1:T(8,128)}, f32[256,256]{0,1:T(8,128)S(1)}, u32[]{:S(2)}, u32[]{:S(2)}) %collective-permute-start.22) | collective-permute-done | bytes 262176 | tf_op jit(solution)/shard_map/ppermute | solution.py:10
  433.9 7.2 %collective-permute-done.23 = f32[256,256]{0,1:T(8,128)S(1)} collective-permute-done((f32[256,256]{0,1:T(8,128)S(1)}, f32[256,256]{0,1:T(8,128)S(1)}, u32[]{:S(2)}, u32[]{:S(2)}) %collective-permute-start.23) | collective-permute-done | bytes 262176 | tf_op jit(solution)/shard_map/ppermute | solution.py:10
  443.4 6.3 %collective-permute-done.24 = f32[256,256]{0,1:T(8,128)S(1)} collective-permute-done((f32[256,256]{0,1:T(8,128)S(1)}, f32[256,256]{0,1:T(8,128)S(1)}, u32[]{:S(2)}, u32[]{:S(2)}) %collective-permute-start.24) | collective-permute-done | bytes 262176 | tf_op jit(solution)/shard_map/ppermute | solution.py:10
  451.3 4.8 collective-permute-done.25
  456.2 3.3 collective-permute-start.26
  459.9 8.0 %collective-permute-done.26 = f32[256,256]{0,1:T(8,128)S(1)} collective-permute-done((f32[256,256]{0,1:T(8,128)S(1)}, f32[256,256]{0,1:T(8,128)S(1)}, u32[]{:S(2)}, u32[]{:S(2)}) %collective-permute-start.26) | collective-permute-done | bytes 262176 | tf_op jit(solution)/shard_map/ppermute | solution.py:10
  467.9 5.8 %collective-permute-start.27 = (f32[256,256]{0,1:T(8,128)S(1)}, f32[256,256]{0,1:T(8,128)S(1)}, u32[]{:S(2)}, u32[]{:S(2)}) collective-permute-start(f32[256,256]{0,1:T(8,128)S(1)} %add.201), channel_id=1, source_target_pairs={{0,128},{4,132},{8,136},{12,140},{16,144},{20,148},{24,152},{28,15... | collective-permute-start | bytes 786440 | tf_op jit(solution)/shard_map/ppermute | solution.py:10
  473.7 3.1 pad_maximum_fusion
  476.8 7.7 %collective-permute-done.27 = f32[256,256]{0,1:T(8,128)S(1)} collective-permute-done((f32[256,256]{0,1:T(8,128)S(1)}, f32[256,256]{0,1:T(8,128)S(1)}, u32[]{:S(2)}, u32[]{:S(2)}) %collective-permute-start.27) | collective-permute-done | bytes 262176 | tf_op jit(solution)/shard_map/ppermute | solution.py:10
  484.7 11.7 %cholesky.240 = f32[128,128]{1,0:T(8,128)S(1)} custom-call(f32[128,128]{1,0:T(8,128)S(1)} %cholesky.276), custom_call_target="Cholesky" | custom-call | tf_op jit(solution)/shard_map/jit(cholesky)/cholesky | solution.py:81
  496.5 9.8 %custom-call.22 = f32[1,128,128]{1,2,0:T(8,128)S(1)} custom-call(f32[1,128,128]{2,1,0:T(8,128)S(1)} %get-tuple-element.59), custom_call_target="InvertDiagBlocksLowerTriangular" | custom-call | tf_op jit(solution)/shard_map/jit(cholesky)/cholesky | solution.py:81
  506.8 11.7 %cholesky.257 = f32[128,128]{1,0:T(8,128)S(1)} custom-call(f32[128,128]{1,0:T(8,128)S(1)} %convolution_subtract_fusion.6), custom_call_target="Cholesky" | custom-call | tf_op jit(solution)/shard_map/jit(cholesky)/cholesky | solution.py:81
  (172 shorter events, 72.7 us)
Async XLA Ops:
  7.2 1.9 copy-start
  7.2 68.5 %all-reduce.11.cloned.1.call-start = ((), (), s32[]{:S(2)}) async-start(), calls=%async_computation.2 | async-start | bytes 1048576 | tf_op jit(solution)/shard_map/psum | solution.py:32
  9.1 2.5 copy-start.13
  11.6 7.1 %copy-start.8 = (f32[2048,256]{1,0:T(8,128)}, f32[2048,256]{1,0:T(8,128)S(1)}, u32[]{:S(2)}) copy-start(f32[2048,256]{1,0:T(8,128)S(1)} %fusion.24) | copy-start | bytes 6291460
  18.8 1.3 copy-start.11
  25.2 211.9 %all-reduce.9.cloned.1.call-start = ((), (), s32[]{:S(2)}) async-start(), calls=%async_computation.1 | async-start | bytes 1572864 | tf_op jit(solution)/shard_map/psum | solution.py:32
  75.7 9.4 %collective-permute-start = (f32[256,256]{0,1:T(8,128)}, f32[256,256]{0,1:T(8,128)S(1)}, u32[]{:S(2)}, u32[]{:S(2)}) collective-permute-start(f32[256,256]{0,1:T(8,128)} %get-tuple-element.46), channel_id=1, source_target_pairs={{0,4},{4,0},{8,12},{12,8},{16,20},{20,16},{24,28},{28,24},{32,36},... | collective-permute-start | bytes 786440 | tf_op jit(solution)/shard_map/ppermute | solution.py:10
  76.3 13.9 %collective-permute-start.4 = (f32[256,256]{1,0:T(8,128)}, f32[256,256]{1,0:T(8,128)S(1)}, u32[]{:S(2)}, u32[]{:S(2)}) collective-permute-start(f32[256,256]{1,0:T(8,128)} %get-tuple-element.47), channel_id=1, source_target_pairs={{0,4},{4,0},{8,12},{12,8},{16,20},{20,16},{24,28},{28,24},{32,36},... | collective-permute-start | bytes 786440 | tf_op jit(solution)/shard_map/ppermute | solution.py:10
  86.1 7.2 %collective-permute-start.1 = (f32[256,256]{0,1:T(8,128)S(1)}, f32[256,256]{0,1:T(8,128)S(1)}, u32[]{:S(2)}, u32[]{:S(2)}) collective-permute-start(f32[256,256]{0,1:T(8,128)S(1)} %add.170), channel_id=1, source_target_pairs={{0,8},{4,12},{8,0},{12,4},{16,24},{20,28},{24,16},{28,20},{32,40},... | collective-permute-start | bytes 786440 | tf_op jit(solution)/shard_map/ppermute | solution.py:10
  91.1 9.3 %collective-permute-start.5 = (f32[256,256]{1,0:T(8,128)S(1)}, f32[256,256]{1,0:T(8,128)S(1)}, u32[]{:S(2)}, u32[]{:S(2)}) collective-permute-start(f32[256,256]{1,0:T(8,128)S(1)} %add.175), channel_id=1, source_target_pairs={{0,8},{4,12},{8,0},{12,4},{16,24},{20,28},{24,16},{28,20},{32,40},... | collective-permute-start | bytes 786440 | tf_op jit(solution)/shard_map/ppermute | solution.py:10
  93.3 13.6 %collective-permute-start.2 = (f32[256,256]{0,1:T(8,128)S(1)}, f32[256,256]{0,1:T(8,128)S(1)}, u32[]{:S(2)}, u32[]{:S(2)}) collective-permute-start(f32[256,256]{0,1:T(8,128)S(1)} %add.171), channel_id=1, source_target_pairs={{0,16},{4,20},{8,24},{12,28},{16,0},{20,4},{24,8},{28,12},{32,48},... | collective-permute-start | bytes 786440 | tf_op jit(solution)/shard_map/ppermute | solution.py:10
  95.6 13.0 %copy-start.9 = (f32[2048,256]{1,0:T(8,128)S(1)}, f32[2048,256]{1,0:T(8,128)}, u32[]{:S(2)}) copy-start(f32[2048,256]{1,0:T(8,128)} %copy-done.8) | copy-start | bytes 6291460
  98.0 10.6 %copy-start.5 = (f32[2048,256]{1,0:T(8,128)}, f32[2048,256]{1,0:T(8,128)S(1)}, u32[]{:S(2)}) copy-start(f32[2048,256]{1,0:T(8,128)S(1)} %fusion) | copy-start | bytes 6291460
  100.4 12.8 %collective-permute-start.6 = (f32[256,256]{1,0:T(8,128)S(1)}, f32[256,256]{1,0:T(8,128)S(1)}, u32[]{:S(2)}, u32[]{:S(2)}) collective-permute-start(f32[256,256]{1,0:T(8,128)S(1)} %add.176), channel_id=1, source_target_pairs={{0,16},{4,20},{8,24},{12,28},{16,0},{20,4},{24,8},{28,12},{32,48},... | collective-permute-start | bytes 786440 | tf_op jit(solution)/shard_map/ppermute | solution.py:10
  106.9 7.0 %collective-permute-start.3 = (f32[256,256]{0,1:T(8,128)S(1)}, f32[256,256]{0,1:T(8,128)S(1)}, u32[]{:S(2)}, u32[]{:S(2)}) collective-permute-start(f32[256,256]{0,1:T(8,128)S(1)} %add.172), channel_id=1, source_target_pairs={{0,32},{4,36},{8,40},{12,44},{16,48},{20,52},{24,56},{28,60},{32,0... | collective-permute-start | bytes 786440 | tf_op jit(solution)/shard_map/ppermute | solution.py:10
  113.3 60.8 %collective-permute-start.7 = (f32[256,256]{1,0:T(8,128)S(1)}, f32[256,256]{1,0:T(8,128)S(1)}, u32[]{:S(2)}, u32[]{:S(2)}) collective-permute-start(f32[256,256]{1,0:T(8,128)S(1)} %add.177), channel_id=1, source_target_pairs={{0,32},{4,36},{8,40},{12,44},{16,48},{20,52},{24,56},{28,60},{32,0... | collective-permute-start | bytes 786440 | tf_op jit(solution)/shard_map/ppermute | solution.py:10
  176.1 4.3 copy-start.12
  180.5 4.3 copy-start.1
  180.5 4.3 copy-start.6
  189.1 234.4 %all-reduce.7.cloned.1.call-start = ((), (), s32[]{:S(2)}) async-start(), calls=%async_computation | async-start | bytes 524288 | tf_op jit(solution)/shard_map/psum | solution.py:32
  237.1 9.4 %collective-permute-start.12 = (f32[256,256]{0,1:T(8,128)}, f32[256,256]{0,1:T(8,128)S(1)}, u32[]{:S(2)}, u32[]{:S(2)}) collective-permute-start(f32[256,256]{0,1:T(8,128)} %get-tuple-element.45), channel_id=1, source_target_pairs={{0,4},{4,0},{8,12},{12,8},{16,20},{20,16},{24,28},{28,24},{32,36},... | collective-permute-start | bytes 786440 | tf_op jit(solution)/shard_map/ppermute | solution.py:10
  237.7 14.4 %collective-permute-start.8 = (f32[256,256]{1,0:T(8,128)}, f32[256,256]{1,0:T(8,128)S(1)}, u32[]{:S(2)}, u32[]{:S(2)}) collective-permute-start(f32[256,256]{1,0:T(8,128)} %get-tuple-element.43), channel_id=1, source_target_pairs={{0,4},{4,0},{8,12},{12,8},{16,20},{20,16},{24,28},{28,24},{32,36},... | collective-permute-start | bytes 786440 | tf_op jit(solution)/shard_map/ppermute | solution.py:10
  239.1 18.0 %collective-permute-start.17 = (f32[256,256]{1,0:T(8,128)}, f32[256,256]{1,0:T(8,128)S(1)}, u32[]{:S(2)}, u32[]{:S(2)}) collective-permute-start(f32[256,256]{1,0:T(8,128)} %get-tuple-element.44), channel_id=1, source_target_pairs={{0,4},{4,0},{8,12},{12,8},{16,20},{20,16},{24,28},{28,24},{32,36},... | collective-permute-start | bytes 786440 | tf_op jit(solution)/shard_map/ppermute | solution.py:10
  247.5 11.3 %collective-permute-start.13 = (f32[256,256]{0,1:T(8,128)S(1)}, f32[256,256]{0,1:T(8,128)S(1)}, u32[]{:S(2)}, u32[]{:S(2)}) collective-permute-start(f32[256,256]{0,1:T(8,128)S(1)} %add.186), channel_id=1, source_target_pairs={{0,8},{4,12},{8,0},{12,4},{16,24},{20,28},{24,16},{28,20},{32,40},... | collective-permute-start | bytes 786440 | tf_op jit(solution)/shard_map/ppermute | solution.py:10
  253.1 8.2 %collective-permute-start.9 = (f32[256,256]{1,0:T(8,128)S(1)}, f32[256,256]{1,0:T(8,128)S(1)}, u32[]{:S(2)}, u32[]{:S(2)}) collective-permute-start(f32[256,256]{1,0:T(8,128)S(1)} %add.182), channel_id=1, source_target_pairs={{0,8},{4,12},{8,0},{12,4},{16,24},{20,28},{24,16},{28,20},{32,40},... | collective-permute-start | bytes 786440 | tf_op jit(solution)/shard_map/ppermute | solution.py:10
  258.1 9.3 %collective-permute-start.18 = (f32[256,256]{1,0:T(8,128)S(1)}, f32[256,256]{1,0:T(8,128)S(1)}, u32[]{:S(2)}, u32[]{:S(2)}) collective-permute-start(f32[256,256]{1,0:T(8,128)S(1)} %add.192), channel_id=1, source_target_pairs={{0,8},{4,12},{8,0},{12,4},{16,24},{20,28},{24,16},{28,20},{32,40},... | collective-permute-start | bytes 786440 | tf_op jit(solution)/shard_map/ppermute | solution.py:10
  258.8 15.1 %collective-permute-start.14 = (f32[256,256]{0,1:T(8,128)S(1)}, f32[256,256]{0,1:T(8,128)S(1)}, u32[]{:S(2)}, u32[]{:S(2)}) collective-permute-start(f32[256,256]{0,1:T(8,128)S(1)} %add.187), channel_id=1, source_target_pairs={{0,16},{4,20},{8,24},{12,28},{16,0},{20,4},{24,8},{28,12},{32,48},... | collective-permute-start | bytes 786440 | tf_op jit(solution)/shard_map/ppermute | solution.py:10
  261.3 18.2 %collective-permute-start.10 = (f32[256,256]{1,0:T(8,128)S(1)}, f32[256,256]{1,0:T(8,128)S(1)}, u32[]{:S(2)}, u32[]{:S(2)}) collective-permute-start(f32[256,256]{1,0:T(8,128)S(1)} %add.183), channel_id=1, source_target_pairs={{0,16},{4,20},{8,24},{12,28},{16,0},{20,4},{24,8},{28,12},{32,48},... | collective-permute-start | bytes 786440 | tf_op jit(solution)/shard_map/ppermute | solution.py:10
  267.4 16.7 %collective-permute-start.19 = (f32[256,256]{1,0:T(8,128)S(1)}, f32[256,256]{1,0:T(8,128)S(1)}, u32[]{:S(2)}, u32[]{:S(2)}) collective-permute-start(f32[256,256]{1,0:T(8,128)S(1)} %add.193), channel_id=1, source_target_pairs={{0,16},{4,20},{8,24},{12,28},{16,0},{20,4},{24,8},{28,12},{32,48},... | collective-permute-start | bytes 786440 | tf_op jit(solution)/shard_map/ppermute | solution.py:10
  274.0 11.8 %collective-permute-start.15 = (f32[256,256]{0,1:T(8,128)S(1)}, f32[256,256]{0,1:T(8,128)S(1)}, u32[]{:S(2)}, u32[]{:S(2)}) collective-permute-start(f32[256,256]{0,1:T(8,128)S(1)} %add.188), channel_id=1, source_target_pairs={{0,32},{4,36},{8,40},{12,44},{16,48},{20,52},{24,56},{28,60},{32,0... | collective-permute-start | bytes 786440 | tf_op jit(solution)/shard_map/ppermute | solution.py:10
  279.6 8.9 %collective-permute-start.11 = (f32[256,256]{1,0:T(8,128)S(1)}, f32[256,256]{1,0:T(8,128)S(1)}, u32[]{:S(2)}, u32[]{:S(2)}) collective-permute-start(f32[256,256]{1,0:T(8,128)S(1)} %add.184), channel_id=1, source_target_pairs={{0,32},{4,36},{8,40},{12,44},{16,48},{20,52},{24,56},{28,60},{32,0... | collective-permute-start | bytes 786440 | tf_op jit(solution)/shard_map/ppermute | solution.py:10
  284.1 13.0 %collective-permute-start.20 = (f32[256,256]{1,0:T(8,128)S(1)}, f32[256,256]{1,0:T(8,128)S(1)}, u32[]{:S(2)}, u32[]{:S(2)}) collective-permute-start(f32[256,256]{1,0:T(8,128)S(1)} %add.194), channel_id=1, source_target_pairs={{0,32},{4,36},{8,40},{12,44},{16,48},{20,52},{24,56},{28,60},{32,0... | collective-permute-start | bytes 786440 | tf_op jit(solution)/shard_map/ppermute | solution.py:10
  285.8 18.0 %collective-permute-start.16 = (f32[256,256]{0,1:T(8,128)S(1)}, f32[256,256]{0,1:T(8,128)}, u32[]{:S(2)}, u32[]{:S(2)}) collective-permute-start(f32[256,256]{0,1:T(8,128)S(1)} %add.189), channel_id=1, source_target_pairs={{0,64},{4,68},{8,72},{12,76},{16,80},{20,84},{24,88},{28,92},{32,9... | collective-permute-start | bytes 786440 | tf_op jit(solution)/shard_map/ppermute | solution.py:10
  297.2 68.5 %collective-permute-start.21 = (f32[256,256]{1,0:T(8,128)S(1)}, f32[256,256]{1,0:T(8,128)S(1)}, u32[]{:S(2)}, u32[]{:S(2)}) collective-permute-start(f32[256,256]{1,0:T(8,128)S(1)} %add.195), channel_id=1, source_target_pairs={{0,64},{4,68},{8,72},{12,76},{16,80},{20,84},{24,88},{28,92},{32,9... | collective-permute-start | bytes 786440 | tf_op jit(solution)/shard_map/ppermute | solution.py:10
  367.8 5.8 %copy-start.7 = (f32[2048,256]{1,0:T(8,128)S(1)}, f32[2048,256]{1,0:T(8,128)}, u32[]{:S(2)}) copy-start(f32[2048,256]{1,0:T(8,128)} %copy-done.5) | copy-start | bytes 6291460
  372.2 1.4 copy-start.3
  423.5 36.0 %copy-start.10 = (f32[2048,256]{1,0:T(8,128)S(1)}, f32[2048,256]{1,0:T(8,128)}, u32[]{:S(2)}) copy-start(f32[2048,256]{1,0:T(8,128)} %copy-done.8) | copy-start | bytes 6291460
  423.5 8.8 %collective-permute-start.22 = (f32[256,256]{0,1:T(8,128)}, f32[256,256]{0,1:T(8,128)S(1)}, u32[]{:S(2)}, u32[]{:S(2)}) collective-permute-start(f32[256,256]{0,1:T(8,128)} %all-reduce.7.cloned.1.call-done), channel_id=1, source_target_pairs={{0,4},{4,0},{8,12},{12,8},{16,20},{20,16},{24,28},{28,24},{32,36},... | collective-permute-start | bytes 786440 | tf_op jit(solution)/shard_map/ppermute | solution.py:10
  433.3 7.8 %collective-permute-start.23 = (f32[256,256]{0,1:T(8,128)S(1)}, f32[256,256]{0,1:T(8,128)S(1)}, u32[]{:S(2)}, u32[]{:S(2)}) collective-permute-start(f32[256,256]{0,1:T(8,128)S(1)} %add.197), channel_id=1, source_target_pairs={{0,8},{4,12},{8,0},{12,4},{16,24},{20,28},{24,16},{28,20},{32,40},... | collective-permute-start | bytes 786440 | tf_op jit(solution)/shard_map/ppermute | solution.py:10
  441.2 8.5 %collective-permute-start.24 = (f32[256,256]{0,1:T(8,128)S(1)}, f32[256,256]{0,1:T(8,128)S(1)}, u32[]{:S(2)}, u32[]{:S(2)}) collective-permute-start(f32[256,256]{0,1:T(8,128)S(1)} %add.198), channel_id=1, source_target_pairs={{0,16},{4,20},{8,24},{12,28},{16,0},{20,4},{24,8},{28,12},{32,48},... | collective-permute-start | bytes 786440 | tf_op jit(solution)/shard_map/ppermute | solution.py:10
  449.7 6.5 %collective-permute-start.25 = (f32[256,256]{0,1:T(8,128)S(1)}, f32[256,256]{0,1:T(8,128)S(1)}, u32[]{:S(2)}, u32[]{:S(2)}) collective-permute-start(f32[256,256]{0,1:T(8,128)S(1)} %add.199), channel_id=1, source_target_pairs={{0,32},{4,36},{8,40},{12,44},{16,48},{20,52},{24,56},{28,60},{32,0... | collective-permute-start | bytes 786440 | tf_op jit(solution)/shard_map/ppermute | solution.py:10
  456.2 17.5 %copy-start.2 = (f32[2048,256]{1,0:T(8,128)S(1)}, f32[2048,256]{1,0:T(8,128)}, u32[]{:S(2)}) copy-start(f32[2048,256]{1,0:T(8,128)} %copy-done.1) | copy-start | bytes 6291460
  456.2 17.5 %copy-start.4 = (f32[2048,256]{1,0:T(8,128)S(1)}, f32[2048,256]{1,0:T(8,128)}, u32[]{:S(2)}) copy-start(f32[2048,256]{1,0:T(8,128)} %copy-done.3) | copy-start | bytes 6291460
  456.2 11.7 %collective-permute-start.26 = (f32[256,256]{0,1:T(8,128)S(1)}, f32[256,256]{0,1:T(8,128)S(1)}, u32[]{:S(2)}, u32[]{:S(2)}) collective-permute-start(f32[256,256]{0,1:T(8,128)S(1)} %add.200), channel_id=1, source_target_pairs={{0,64},{4,68},{8,72},{12,76},{16,80},{20,84},{24,88},{28,92},{32,9... | collective-permute-start | bytes 786440 | tf_op jit(solution)/shard_map/ppermute | solution.py:10
  467.9 16.6 %collective-permute-start.27 = (f32[256,256]{0,1:T(8,128)S(1)}, f32[256,256]{0,1:T(8,128)S(1)}, u32[]{:S(2)}, u32[]{:S(2)}) collective-permute-start(f32[256,256]{0,1:T(8,128)S(1)} %add.201), channel_id=1, source_target_pairs={{0,128},{4,132},{8,136},{12,140},{16,144},{20,148},{24,152},{28,15... | collective-permute-start | bytes 786440 | tf_op jit(solution)/shard_map/ppermute | solution.py:10
Sparse Core Ops, SparseCore 0:
  25.3 50.3 all-reduce.10
  189.2 47.8 all-reduce.8
  378.0 45.4 all-reduce.6
where the time goes:
time: 538 us; the launch traced here: 529 us
  waiting for transfers between devices  241 us (45%)
  other arithmetic  155 us (29%)
  matrix products  55.8 us (10%)
  starting transfers between devices  44.3 us (8%)
  between operations  18.6 us (3%)
  local copies, waits for them, and re-layouts  14 us (3%)
    psum x3, waiting for transfers between devices, group_total(): summed = lax.psum(partial_value, 'rows')  144 us
    another operation x20, other arithmetic, on_device(): jnp.linalg.cholesky(identity + gram_matrix / node_rows[level_index])  104 us
    ppermute x28, waiting for transfers between devices, partner(): lax.ppermute(value, axis, [(i, i ^ 1 << bit) for i in range(lax.axis_size...  96.5 us
    ppermute x28, starting transfers between devices, partner(): lax.ppermute(value, axis, [(i, i ^ 1 << bit) for i in range(lax.axis_size...  44.2 us
    another operation x3, other arithmetic, solve_with(): return jax.scipy.linalg.cho_solve((factor, True), right_side)  39.6 us
    dot_general x6, matrix products, project(): jnp.einsum('nr,ns->rs', left, right, precision=highest, preferred_element...  27.2 us
    dot_general x3, matrix products, on_device(): jnp.dot(bases[prior_index], coefficients[prior_index, level_index], preci...  14.2 us
  transfers between devices with their start and end apart: 31, of which 22 were waited for; matrix products, arithmetic and copies ran while one was open for 27% of the time, Pallas kernels for 0%

commit v1 on v0

--- a/solution.py
+++ b/solution.py
@@ -29,7 +29,7 @@
 
 
 def group_total(partial_value, width_bits):
-    summed = lax.psum(partial_value, "rows")
+    summed = jnp.sum(lax.all_gather(partial_value, "rows"), axis=0)
     for bit_index in range(width_bits):
         summed = summed + partner(summed, "branch", bit_index)
     return summed

time: 538 us -> 483 us (0.90)
  waiting for transfers between devices: 241 us -> 187 us
    psum x3 -> x0, waiting for transfers between devices: 144 us -> none  [group_total(): summed = lax.psum(partial_value, 'rows')]
    all_gather x0 -> x6, waiting for transfers between devices: none -> 70.4 us  [group_total(): summed = jnp.sum(lax.all_gather(partial_value, 'rows'), axis=0)]
    ppermute x28, waiting for transfers between devices: 96.5 us -> 116 us  [partner(): lax.ppermute(value, axis, [(i, i ^ 1 << bit) for i in range(lax.axis_size...]
    reduce_sum x0 -> x6, other arithmetic: none -> 7.94 us  [group_total(): summed = jnp.sum(lax.all_gather(partial_value, 'rows'), axis=0)]
  transfers between devices with their start and end apart: 31 -> 34, of which waited for: 22 -> 23; matrix products, arithmetic and copies ran while one was open for 27% -> 35% of each run, Pallas kernels for 0% -> 0%
where the time goes in v1:
time: 483 us; the launch traced here: 478 us
  waiting for transfers between devices  187 us (39%)
  other arithmetic  158 us (33%)
  matrix products  57.3 us (12%)
  starting transfers between devices  40.4 us (8%)
  between operations  19 us (4%)
  local copies, waits for them, and re-layouts  16.2 us (3%)
    ppermute x28, waiting for transfers between devices, partner(): lax.ppermute(value, axis, [(i, i ^ 1 << bit) for i in range(lax.axis_size...  116 us
    another operation x20, other arithmetic, on_device(): jnp.linalg.cholesky(identity + gram_matrix / node_rows[level_index])  103 us
    all_gather x6, waiting for transfers between devices, group_total(): summed = jnp.sum(lax.all_gather(partial_value, 'rows'), axis=0)  70.4 us
    ppermute x28, starting transfers between devices, partner(): lax.ppermute(value, axis, [(i, i ^ 1 << bit) for i in range(lax.axis_size...  39.7 us
    another operation x3, other arithmetic, solve_with(): return jax.scipy.linalg.cho_solve((factor, True), right_side)  39.4 us
    dot_general x6, matrix products, project(): jnp.einsum('nr,ns->rs', left, right, precision=highest, preferred_element...  28.8 us
    dot_general x3, matrix products, on_device(): jnp.dot(bases[prior_index], coefficients[prior_index, level_index], preci...  14.1 us
  transfers between devices with their start and end apart: 34, of which 23 were waited for; matrix products, arithmetic and copies ran while one was open for 35% of the time, Pallas kernels for 0%

profile of v1, /device:TPU:8, one launch (start us, length us, event | category | flops | bytes accessed | tf_op | source)
XLA Modules:
  0.0 477.8 jit_solution(7492827573289778706)
XLA Ops:
  12.9 4.6 fusion.127
  21.6 4.6 fusion.126
  26.3 17.6 %all-gather.13.cloned.1.call-done = f32[1024,256]{1,0:T(8,128)} async-done(((f32[256,256]{1,0:T(8,128)}), f32[1024,256]{1,0:T(8,128)}) %all-gather.13.cloned.1.call-update) | async-done | bytes 1048592 | tf_op jit(solution)/shard_map/all_gather | solution.py:32
  46.0 23.1 %all-gather.15.cloned.1.call-done = f32[1024,256]{1,0:T(8,128)} async-done(((f32[256,256]{1,0:T(8,128)}), f32[1024,256]{1,0:T(8,128)}) %all-gather.15.cloned.1.call-update) | async-done | bytes 1048592 | tf_op jit(solution)/shard_map/all_gather | solution.py:32
  71.7 7.2 %collective-permute-done.4 = f32[256,256]{1,0:T(8,128)S(1)} collective-permute-done((f32[256,256]{1,0:T(8,128)S(1)}, f32[256,256]{1,0:T(8,128)S(1)}, u32[]{:S(2)}, u32[]{:S(2)}) %collective-permute-start.4) | collective-permute-done | bytes 262176 | tf_op jit(solution)/shard_map/ppermute | solution.py:10
  84.8 3.4 collective-permute-done.5
  90.5 4.3 collective-permute-done.2
  96.5 4.6 fusion.125
  102.4 11.7 %cholesky.172 = f32[128,128]{1,0:T(8,128)S(1)} custom-call(f32[128,128]{1,0:T(8,128)S(1)} %cholesky.270), custom_call_target="Cholesky" | custom-call | tf_op jit(solution)/shard_map/jit(cholesky)/cholesky | solution.py:81
  114.2 9.8 %custom-call.17 = f32[1,128,128]{1,2,0:T(8,128)S(1)} custom-call(f32[1,128,128]{2,1,0:T(8,128)S(1)} %get-tuple-element.62), custom_call_target="InvertDiagBlocksLowerTriangular" | custom-call | tf_op jit(solution)/shard_map/jit(cholesky)/cholesky | solution.py:81
  124.5 11.7 %cholesky.189 = f32[128,128]{1,0:T(8,128)S(1)} custom-call(f32[128,128]{1,0:T(8,128)S(1)} %convolution_subtract_fusion.8), custom_call_target="Cholesky" | custom-call | tf_op jit(solution)/shard_map/jit(cholesky)/cholesky | solution.py:81
  138.3 4.2 while.6
  142.5 19.7 %custom-call.18 = f32[2,128,128]{1,2,0:T(8,128)S(1)} custom-call(f32[2,128,128]{2,1,0:T(8,128)S(1)} %get-tuple-element.24), custom_call_target="InvertDiagBlocksLowerTriangular" | custom-call | tf_op jit(solution)/shard_map/jit(_cho_solve)/triangular_solve | solution.py:28
  164.3 4.3 convolution_subtract_fusion.2
  169.9 4.3 fusion.132
  174.5 6.4 %fusion.133 = f32[256,256]{1,0:T(8,128)} fusion(f32[2048,256]{1,0:T(8,128)} %copy-done.1, f32[2048,256]{1,0:T(8,128)} %copy-done.5), kind=kOutput, calls=%fused_computation.202 | convolution fusion | flops 1610612736 | bytes 4456448 | tf_op jit(solution)/shard_map/nr,ns->rs/dot_general | solution.py:22
  182.9 8.0 %collective-permute-done.8 = f32[256,256]{1,0:T(8,128)S(1)} collective-permute-done((f32[256,256]{1,0:T(8,128)S(1)}, f32[256,256]{1,0:T(8,128)S(1)}, u32[]{:S(2)}, u32[]{:S(2)}) %collective-permute-start.8) | collective-permute-done | bytes 262176 | tf_op jit(solution)/shard_map/ppermute | solution.py:10
  191.0 4.4 collective-permute-start.9
  195.4 4.4 collective-permute-done.9
  199.9 7.9 %collective-permute-done.10 = f32[256,256]{1,0:T(8,128)S(1)} collective-permute-done((f32[256,256]{1,0:T(8,128)S(1)}, f32[256,256]{1,0:T(8,128)S(1)}, u32[]{:S(2)}, u32[]{:S(2)}) %collective-permute-start.10) | collective-permute-done | bytes 262176 | tf_op jit(solution)/shard_map/ppermute | solution.py:10
  215.3 8.2 %all-gather.21.cloned.1.call-done = f32[1024,256]{1,0:T(8,128)} async-done(((f32[256,256]{1,0:T(8,128)}), f32[1024,256]{1,0:T(8,128)}) %all-gather.21.cloned.1.call-update) | async-done | bytes 1048592 | tf_op jit(solution)/shard_map/all_gather | solution.py:32
  226.8 6.5 %collective-permute-done.17 = f32[256,256]{1,0:T(8,128)S(1)} collective-permute-done((f32[256,256]{1,0:T(8,128)S(1)}, f32[256,256]{1,0:T(8,128)S(1)}, u32[]{:S(2)}, u32[]{:S(2)}) %collective-permute-start.17) | collective-permute-done | bytes 262176 | tf_op jit(solution)/shard_map/ppermute | solution.py:10
  235.4 7.3 %collective-permute-done.18 = f32[256,256]{1,0:T(8,128)S(1)} collective-permute-done((f32[256,256]{1,0:T(8,128)S(1)}, f32[256,256]{1,0:T(8,128)S(1)}, u32[]{:S(2)}, u32[]{:S(2)}) %collective-permute-start.18) | collective-permute-done | bytes 262176 | tf_op jit(solution)/shard_map/ppermute | solution.py:10
  242.8 4.6 collective-permute-done.14
  252.3 6.3 %collective-permute-done.15 = f32[256,256]{0,1:T(8,128)} collective-permute-done((f32[256,256]{0,1:T(8,128)S(1)}, f32[256,256]{0,1:T(8,128)}, u32[]{:S(2)}, u32[]{:S(2)}) %collective-permute-start.15) | collective-permute-done | bytes 262176 | tf_op jit(solution)/shard_map/ppermute | solution.py:10
  259.6 5.4 %convolution_subtract_fusion.1 = f32[2048,256]{1,0:T(8,128)} fusion(f32[2048,256]{1,0:T(8,128)} %copy-done.5, f32[2048]{0:T(1024)S(1)} %copy-done.13, f32[128,256]{0,1:T(8,128)S(1)} %copy.16, f32[128,256]{0,1:T(8,128)S(1)} %fusion.103, f32[2048,256]{1,0:T(8,128)} %copy-done.7), kind=kOutput, calls=%fused_computation.6 | convolution fusion | flops 1612316672 | bytes 6561792 | tf_op jit(solution)/shard_map/dot_general | solution.py:73
  265.0 3.5 collective-permute-start.21
  268.5 9.8 %collective-permute-done.16 = f32[256,256]{0,1:T(8,128)S(1)} collective-permute-done((f32[256,256]{0,1:T(8,128)S(1)}, f32[256,256]{0,1:T(8,128)S(1)}, u32[]{:S(2)}, u32[]{:S(2)}) %collective-permute-start.16) | collective-permute-done | bytes 262176 | tf_op jit(solution)/shard_map/ppermute | solution.py:10
  278.5 11.7 %cholesky.206 = f32[128,128]{1,0:T(8,128)S(1)} custom-call(f32[128,128]{1,0:T(8,128)S(1)} %cholesky.273), custom_call_target="Cholesky" | custom-call | tf_op jit(solution)/shard_map/jit(cholesky)/cholesky | solution.py:81
  290.3 9.8 %custom-call.20 = f32[1,128,128]{1,2,0:T(8,128)S(1)} custom-call(f32[1,128,128]{2,1,0:T(8,128)S(1)} %get-tuple-element.58), custom_call_target="InvertDiagBlocksLowerTriangular" | custom-call | tf_op jit(solution)/shard_map/jit(cholesky)/cholesky | solution.py:81
  300.6 11.7 %cholesky.223 = f32[128,128]{1,0:T(8,128)S(1)} custom-call(f32[128,128]{1,0:T(8,128)S(1)} %convolution_subtract_fusion.7), custom_call_target="Cholesky" | custom-call | tf_op jit(solution)/shard_map/jit(cholesky)/cholesky | solution.py:81
  315.0 4.2 while.7
  319.1 19.7 %custom-call.21 = f32[2,128,128]{1,2,0:T(8,128)S(1)} custom-call(f32[2,128,128]{2,1,0:T(8,128)S(1)} %get-tuple-element.26), custom_call_target="InvertDiagBlocksLowerTriangular" | custom-call | tf_op jit(solution)/shard_map/jit(_cho_solve)/triangular_solve | solution.py:28
  340.9 4.4 convolution_subtract_fusion
  346.6 4.3 fusion.134
  350.9 21.6 %all-gather.23.cloned.1.call-done = f32[1024,256]{1,0:T(8,128)} async-done(((f32[256,256]{1,0:T(8,128)}), f32[1024,256]{1,0:T(8,128)}) %all-gather.23.cloned.1.call-update) | async-done | bytes 1048592 | tf_op jit(solution)/shard_map/all_gather | solution.py:32
  374.6 7.9 %collective-permute-done.22 = f32[256,256]{0,1:T(8,128)S(1)} collective-permute-done((f32[256,256]{0,1:T(8,128)S(1)}, f32[256,256]{0,1:T(8,128)S(1)}, u32[]{:S(2)}, u32[]{:S(2)}) %collective-permute-start.22) | collective-permute-done | bytes 262176 | tf_op jit(solution)/shard_map/ppermute | solution.py:10
  383.2 7.0 %collective-permute-done.23 = f32[256,256]{0,1:T(8,128)S(1)} collective-permute-done((f32[256,256]{0,1:T(8,128)S(1)}, f32[256,256]{0,1:T(8,128)S(1)}, u32[]{:S(2)}, u32[]{:S(2)}) %collective-permute-start.23) | collective-permute-done | bytes 262176 | tf_op jit(solution)/shard_map/ppermute | solution.py:10
  392.4 6.1 %collective-permute-done.24 = f32[256,256]{0,1:T(8,128)S(1)} collective-permute-done((f32[256,256]{0,1:T(8,128)S(1)}, f32[256,256]{0,1:T(8,128)S(1)}, u32[]{:S(2)}, u32[]{:S(2)}) %collective-permute-start.24) | collective-permute-done | bytes 262176 | tf_op jit(solution)/shard_map/ppermute | solution.py:10
  400.2 4.8 %collective-permute-done.25 = f32[256,256]{0,1:T(8,128)S(1)} collective-permute-done((f32[256,256]{0,1:T(8,128)S(1)}, f32[256,256]{0,1:T(8,128)S(1)}, u32[]{:S(2)}, u32[]{:S(2)}) %collective-permute-start.25) | collective-permute-done | bytes 262176 | tf_op jit(solution)/shard_map/ppermute | solution.py:10
  405.1 3.5 collective-permute-start.26
  408.9 7.7 %collective-permute-done.26 = f32[256,256]{0,1:T(8,128)S(1)} collective-permute-done((f32[256,256]{0,1:T(8,128)S(1)}, f32[256,256]{0,1:T(8,128)S(1)}, u32[]{:S(2)}, u32[]{:S(2)}) %collective-permute-start.26) | collective-permute-done | bytes 262176 | tf_op jit(solution)/shard_map/ppermute | solution.py:10
  416.7 5.8 %collective-permute-start.27 = (f32[256,256]{0,1:T(8,128)S(1)}, f32[256,256]{0,1:T(8,128)S(1)}, u32[]{:S(2)}, u32[]{:S(2)}) collective-permute-start(f32[256,256]{0,1:T(8,128)S(1)} %add.189), channel_id=1, source_target_pairs={{0,128},{4,132},{8,136},{12,140},{16,144},{20,148},{24,152},{28,15... | collective-permute-start | bytes 786440 | tf_op jit(solution)/shard_map/ppermute | solution.py:10
  422.5 3.1 pad_maximum_fusion
  425.6 7.5 %collective-permute-done.27 = f32[256,256]{0,1:T(8,128)S(1)} collective-permute-done((f32[256,256]{0,1:T(8,128)S(1)}, f32[256,256]{0,1:T(8,128)S(1)}, u32[]{:S(2)}, u32[]{:S(2)}) %collective-permute-start.27) | collective-permute-done | bytes 262176 | tf_op jit(solution)/shard_map/ppermute | solution.py:10
  433.4 11.7 %cholesky.240 = f32[128,128]{1,0:T(8,128)S(1)} custom-call(f32[128,128]{1,0:T(8,128)S(1)} %cholesky.276), custom_call_target="Cholesky" | custom-call | tf_op jit(solution)/shard_map/jit(cholesky)/cholesky | solution.py:81
  445.2 9.8 %custom-call.22 = f32[1,128,128]{1,2,0:T(8,128)S(1)} custom-call(f32[1,128,128]{2,1,0:T(8,128)S(1)} %get-tuple-element.54), custom_call_target="InvertDiagBlocksLowerTriangular" | custom-call | tf_op jit(solution)/shard_map/jit(cholesky)/cholesky | solution.py:81
  455.5 11.7 %cholesky.257 = f32[128,128]{1,0:T(8,128)S(1)} custom-call(f32[128,128]{1,0:T(8,128)S(1)} %convolution_subtract_fusion.6), custom_call_target="Cholesky" | custom-call | tf_op jit(solution)/shard_map/jit(cholesky)/cholesky | solution.py:81
  (190 shorter events, 75.0 us)
Async XLA Ops:
  7.2 1.9 copy-start
  7.2 36.7 %all-gather.13.cloned.1.call-start = ((), (), s32[]{:S(2)}) async-start(), calls=%async_computation | async-start | bytes 1310720 | tf_op jit(solution)/shard_map/all_gather | solution.py:32
  9.1 3.8 copy-start.13
  11.6 1.3 copy-start.7
  17.6 51.5 %all-gather.15.cloned.1.call-start = ((), (), s32[]{:S(2)}) async-start(), calls=%async_computation.1 | async-start | bytes 1310720 | tf_op jit(solution)/shard_map/all_gather | solution.py:32
  17.8 3.8 copy-start.8
  20.3 1.3 copy-start.11
  26.3 154.7 %all-gather.17.cloned.1.call-start = ((), (), s32[]{:S(2)}) async-start(), calls=%async_computation.2 | async-start | bytes 1310720 | tf_op jit(solution)/shard_map/all_gather | solution.py:32
  45.4 25.7 %collective-permute-start = (f32[256,256]{0,1:T(8,128)S(1)}, f32[256,256]{0,1:T(8,128)S(1)}, u32[]{:S(2)}, u32[]{:S(2)}) collective-permute-start(f32[256,256]{0,1:T(8,128)S(1)} %copy.13), channel_id=1, source_target_pairs={{0,4},{4,0},{8,12},{12,8},{16,20},{20,16},{24,28},{28,24},{32,36},... | collective-permute-start | bytes 786440 | tf_op jit(solution)/shard_map/ppermute | solution.py:10
  70.4 8.5 %collective-permute-start.4 = (f32[256,256]{1,0:T(8,128)S(1)}, f32[256,256]{1,0:T(8,128)S(1)}, u32[]{:S(2)}, u32[]{:S(2)}) collective-permute-start(f32[256,256]{1,0:T(8,128)S(1)} %reduce_sum.55), channel_id=1, source_target_pairs={{0,4},{4,0},{8,12},{12,8},{16,20},{20,16},{24,28},{28,24},{32,36},... | collective-permute-start | bytes 786440 | tf_op jit(solution)/shard_map/ppermute | solution.py:10
  71.1 8.5 %collective-permute-start.1 = (f32[256,256]{0,1:T(8,128)S(1)}, f32[256,256]{0,1:T(8,128)S(1)}, u32[]{:S(2)}, u32[]{:S(2)}) collective-permute-start(f32[256,256]{0,1:T(8,128)S(1)} %add.158), channel_id=1, source_target_pairs={{0,8},{4,12},{8,0},{12,4},{16,24},{20,28},{24,16},{28,20},{32,40},... | collective-permute-start | bytes 786440 | tf_op jit(solution)/shard_map/ppermute | solution.py:10
  79.0 9.3 %collective-permute-start.5 = (f32[256,256]{1,0:T(8,128)S(1)}, f32[256,256]{1,0:T(8,128)S(1)}, u32[]{:S(2)}, u32[]{:S(2)}) collective-permute-start(f32[256,256]{1,0:T(8,128)S(1)} %add.163), channel_id=1, source_target_pairs={{0,8},{4,12},{8,0},{12,4},{16,24},{20,28},{24,16},{28,20},{32,40},... | collective-permute-start | bytes 786440 | tf_op jit(solution)/shard_map/ppermute | solution.py:10
  79.6 15.1 %collective-permute-start.2 = (f32[256,256]{0,1:T(8,128)S(1)}, f32[256,256]{0,1:T(8,128)S(1)}, u32[]{:S(2)}, u32[]{:S(2)}) collective-permute-start(f32[256,256]{0,1:T(8,128)S(1)} %add.159), channel_id=1, source_target_pairs={{0,16},{4,20},{8,24},{12,28},{16,0},{20,4},{24,8},{28,12},{32,48},... | collective-permute-start | bytes 786440 | tf_op jit(solution)/shard_map/ppermute | solution.py:10
  82.3 14.1 %copy-start.9 = (f32[2048,256]{1,0:T(8,128)S(1)}, f32[2048,256]{1,0:T(8,128)}, u32[]{:S(2)}) copy-start(f32[2048,256]{1,0:T(8,128)} %copy-done.7) | copy-start | bytes 6291460
  84.8 11.6 %copy-start.5 = (f32[2048,256]{1,0:T(8,128)}, f32[2048,256]{1,0:T(8,128)S(1)}, u32[]{:S(2)}) copy-start(f32[2048,256]{1,0:T(8,128)S(1)} %fusion) | copy-start | bytes 6291460
  88.3 12.9 %collective-permute-start.6 = (f32[256,256]{1,0:T(8,128)S(1)}, f32[256,256]{1,0:T(8,128)S(1)}, u32[]{:S(2)}, u32[]{:S(2)}) collective-permute-start(f32[256,256]{1,0:T(8,128)S(1)} %add.164), channel_id=1, source_target_pairs={{0,16},{4,20},{8,24},{12,28},{16,0},{20,4},{24,8},{28,12},{32,48},... | collective-permute-start | bytes 786440 | tf_op jit(solution)/shard_map/ppermute | solution.py:10
  94.8 7.4 %collective-permute-start.3 = (f32[256,256]{0,1:T(8,128)S(1)}, f32[256,256]{0,1:T(8,128)S(1)}, u32[]{:S(2)}, u32[]{:S(2)}) collective-permute-start(f32[256,256]{0,1:T(8,128)S(1)} %add.160), channel_id=1, source_target_pairs={{0,32},{4,36},{8,40},{12,44},{16,48},{20,52},{24,56},{28,60},{32,0... | collective-permute-start | bytes 786440 | tf_op jit(solution)/shard_map/ppermute | solution.py:10
  101.1 108.4 %all-gather.19.cloned.1.call-start = ((), (), s32[]{:S(2)}) async-start(), calls=%async_computation.3 | async-start | bytes 1310720 | tf_op jit(solution)/shard_map/all_gather | solution.py:32
  101.2 61.0 %collective-permute-start.7 = (f32[256,256]{1,0:T(8,128)S(1)}, f32[256,256]{1,0:T(8,128)S(1)}, u32[]{:S(2)}, u32[]{:S(2)}) collective-permute-start(f32[256,256]{1,0:T(8,128)S(1)} %add.165), channel_id=1, source_target_pairs={{0,32},{4,36},{8,40},{12,44},{16,48},{20,52},{24,56},{28,60},{32,0... | collective-permute-start | bytes 786440 | tf_op jit(solution)/shard_map/ppermute | solution.py:10
  164.3 5.6 %copy-start.12 = (f32[2048,256]{1,0:T(8,128)S(1)}, f32[2048,256]{1,0:T(8,128)}, u32[]{:S(2)}) copy-start(f32[2048,256]{1,0:T(8,128)} %copy-done.11) | copy-start | bytes 6291460
  168.6 1.3 copy-start.1
  174.2 49.3 %all-gather.21.cloned.1.call-start = ((), (), s32[]{:S(2)}) async-start(), calls=%async_computation.4 | async-start | bytes 1310720 | tf_op jit(solution)/shard_map/all_gather | solution.py:32
  180.9 191.6 %all-gather.23.cloned.1.call-start = ((), (), s32[]{:S(2)}) async-start(), calls=%async_computation.5 | async-start | bytes 1310720 | tf_op jit(solution)/shard_map/all_gather | solution.py:32
  182.3 8.7 %collective-permute-start.8 = (f32[256,256]{1,0:T(8,128)S(1)}, f32[256,256]{1,0:T(8,128)S(1)}, u32[]{:S(2)}, u32[]{:S(2)}) collective-permute-start(f32[256,256]{1,0:T(8,128)S(1)} %reduce_sum.56), channel_id=1, source_target_pairs={{0,4},{4,0},{8,12},{12,8},{16,20},{20,16},{24,28},{28,24},{32,36},... | collective-permute-start | bytes 786440 | tf_op jit(solution)/shard_map/ppermute | solution.py:10
  191.0 8.7 %collective-permute-start.9 = (f32[256,256]{1,0:T(8,128)S(1)}, f32[256,256]{1,0:T(8,128)S(1)}, u32[]{:S(2)}, u32[]{:S(2)}) collective-permute-start(f32[256,256]{1,0:T(8,128)S(1)} %add.170), channel_id=1, source_target_pairs={{0,8},{4,12},{8,0},{12,4},{16,24},{20,28},{24,16},{28,20},{32,40},... | collective-permute-start | bytes 786440 | tf_op jit(solution)/shard_map/ppermute | solution.py:10
  199.8 8.0 %collective-permute-start.10 = (f32[256,256]{1,0:T(8,128)S(1)}, f32[256,256]{1,0:T(8,128)S(1)}, u32[]{:S(2)}, u32[]{:S(2)}) collective-permute-start(f32[256,256]{1,0:T(8,128)S(1)} %add.171), channel_id=1, source_target_pairs={{0,16},{4,20},{8,24},{12,28},{16,0},{20,4},{24,8},{28,12},{32,48},... | collective-permute-start | bytes 786440 | tf_op jit(solution)/shard_map/ppermute | solution.py:10
  207.8 6.6 %collective-permute-start.11 = (f32[256,256]{1,0:T(8,128)S(1)}, f32[256,256]{1,0:T(8,128)}, u32[]{:S(2)}, u32[]{:S(2)}) collective-permute-start(f32[256,256]{1,0:T(8,128)S(1)} %add.172), channel_id=1, source_target_pairs={{0,32},{4,36},{8,40},{12,44},{16,48},{20,52},{24,56},{28,60},{32,0... | collective-permute-start | bytes 786440 | tf_op jit(solution)/shard_map/ppermute | solution.py:10
  210.9 14.2 %collective-permute-start.12 = (f32[256,256]{0,1:T(8,128)S(1)}, f32[256,256]{0,1:T(8,128)S(1)}, u32[]{:S(2)}, u32[]{:S(2)}) collective-permute-start(f32[256,256]{0,1:T(8,128)S(1)} %copy.18), channel_id=1, source_target_pairs={{0,4},{4,0},{8,12},{12,8},{16,20},{20,16},{24,28},{28,24},{32,36},... | collective-permute-start | bytes 786440 | tf_op jit(solution)/shard_map/ppermute | solution.py:10
  224.8 8.5 %collective-permute-start.17 = (f32[256,256]{1,0:T(8,128)S(1)}, f32[256,256]{1,0:T(8,128)S(1)}, u32[]{:S(2)}, u32[]{:S(2)}) collective-permute-start(f32[256,256]{1,0:T(8,128)S(1)} %reduce_sum.58), channel_id=1, source_target_pairs={{0,4},{4,0},{8,12},{12,8},{16,20},{20,16},{24,28},{28,24},{32,36},... | collective-permute-start | bytes 786440 | tf_op jit(solution)/shard_map/ppermute | solution.py:10
  225.2 8.6 %collective-permute-start.13 = (f32[256,256]{0,1:T(8,128)S(1)}, f32[256,256]{0,1:T(8,128)S(1)}, u32[]{:S(2)}, u32[]{:S(2)}) collective-permute-start(f32[256,256]{0,1:T(8,128)S(1)} %add.174), channel_id=1, source_target_pairs={{0,8},{4,12},{8,0},{12,4},{16,24},{20,28},{24,16},{28,20},{32,40},... | collective-permute-start | bytes 786440 | tf_op jit(solution)/shard_map/ppermute | solution.py:10
  233.4 9.3 %collective-permute-start.18 = (f32[256,256]{1,0:T(8,128)S(1)}, f32[256,256]{1,0:T(8,128)S(1)}, u32[]{:S(2)}, u32[]{:S(2)}) collective-permute-start(f32[256,256]{1,0:T(8,128)S(1)} %add.180), channel_id=1, source_target_pairs={{0,8},{4,12},{8,0},{12,4},{16,24},{20,28},{24,16},{28,20},{32,40},... | collective-permute-start | bytes 786440 | tf_op jit(solution)/shard_map/ppermute | solution.py:10
  233.9 13.5 %collective-permute-start.14 = (f32[256,256]{0,1:T(8,128)S(1)}, f32[256,256]{0,1:T(8,128)S(1)}, u32[]{:S(2)}, u32[]{:S(2)}) collective-permute-start(f32[256,256]{0,1:T(8,128)S(1)} %add.175), channel_id=1, source_target_pairs={{0,16},{4,20},{8,24},{12,28},{16,0},{20,4},{24,8},{28,12},{32,48},... | collective-permute-start | bytes 786440 | tf_op jit(solution)/shard_map/ppermute | solution.py:10
  242.7 8.7 %collective-permute-start.19 = (f32[256,256]{1,0:T(8,128)S(1)}, f32[256,256]{1,0:T(8,128)S(1)}, u32[]{:S(2)}, u32[]{:S(2)}) collective-permute-start(f32[256,256]{1,0:T(8,128)S(1)} %add.181), channel_id=1, source_target_pairs={{0,16},{4,20},{8,24},{12,28},{16,0},{20,4},{24,8},{28,12},{32,48},... | collective-permute-start | bytes 786440 | tf_op jit(solution)/shard_map/ppermute | solution.py:10
  247.5 11.0 %collective-permute-start.15 = (f32[256,256]{0,1:T(8,128)S(1)}, f32[256,256]{0,1:T(8,128)}, u32[]{:S(2)}, u32[]{:S(2)}) collective-permute-start(f32[256,256]{0,1:T(8,128)S(1)} %add.176), channel_id=1, source_target_pairs={{0,32},{4,36},{8,40},{12,44},{16,48},{20,52},{24,56},{28,60},{32,0... | collective-permute-start | bytes 786440 | tf_op jit(solution)/shard_map/ppermute | solution.py:10
  251.5 13.5 %collective-permute-start.20 = (f32[256,256]{1,0:T(8,128)S(1)}, f32[256,256]{1,0:T(8,128)S(1)}, u32[]{:S(2)}, u32[]{:S(2)}) collective-permute-start(f32[256,256]{1,0:T(8,128)S(1)} %add.182), channel_id=1, source_target_pairs={{0,32},{4,36},{8,40},{12,44},{16,48},{20,52},{24,56},{28,60},{32,0... | collective-permute-start | bytes 786440 | tf_op jit(solution)/shard_map/ppermute | solution.py:10
  259.5 18.8 %collective-permute-start.16 = (f32[256,256]{0,1:T(8,128)S(1)}, f32[256,256]{0,1:T(8,128)S(1)}, u32[]{:S(2)}, u32[]{:S(2)}) collective-permute-start(f32[256,256]{0,1:T(8,128)S(1)} %add.177), channel_id=1, source_target_pairs={{0,64},{4,68},{8,72},{12,76},{16,80},{20,84},{24,88},{28,92},{32,9... | collective-permute-start | bytes 786440 | tf_op jit(solution)/shard_map/ppermute | solution.py:10
  265.0 73.8 %collective-permute-start.21 = (f32[256,256]{1,0:T(8,128)S(1)}, f32[256,256]{1,0:T(8,128)S(1)}, u32[]{:S(2)}, u32[]{:S(2)}) collective-permute-start(f32[256,256]{1,0:T(8,128)S(1)} %add.183), channel_id=1, source_target_pairs={{0,64},{4,68},{8,72},{12,76},{16,80},{20,84},{24,88},{28,92},{32,9... | collective-permute-start | bytes 786440 | tf_op jit(solution)/shard_map/ppermute | solution.py:10
  340.9 5.7 %copy-start.6 = (f32[2048,256]{1,0:T(8,128)S(1)}, f32[2048,256]{1,0:T(8,128)}, u32[]{:S(2)}) copy-start(f32[2048,256]{1,0:T(8,128)} %copy-done.5) | copy-start | bytes 6291460
  345.3 1.3 copy-start.3
  374.0 34.6 %copy-start.10 = (f32[2048,256]{1,0:T(8,128)S(1)}, f32[2048,256]{1,0:T(8,128)}, u32[]{:S(2)}) copy-start(f32[2048,256]{1,0:T(8,128)} %copy-done.7) | copy-start | bytes 6291460
  374.0 8.5 %collective-permute-start.22 = (f32[256,256]{0,1:T(8,128)S(1)}, f32[256,256]{0,1:T(8,128)S(1)}, u32[]{:S(2)}, u32[]{:S(2)}) collective-permute-start(f32[256,256]{0,1:T(8,128)S(1)} %copy.22), channel_id=1, source_target_pairs={{0,4},{4,0},{8,12},{12,8},{16,20},{20,16},{24,28},{28,24},{32,36},... | collective-permute-start | bytes 786440 | tf_op jit(solution)/shard_map/ppermute | solution.py:10
  382.5 7.7 %collective-permute-start.23 = (f32[256,256]{0,1:T(8,128)S(1)}, f32[256,256]{0,1:T(8,128)S(1)}, u32[]{:S(2)}, u32[]{:S(2)}) collective-permute-start(f32[256,256]{0,1:T(8,128)S(1)} %add.185), channel_id=1, source_target_pairs={{0,8},{4,12},{8,0},{12,4},{16,24},{20,28},{24,16},{28,20},{32,40},... | collective-permute-start | bytes 786440 | tf_op jit(solution)/shard_map/ppermute | solution.py:10
  390.2 8.3 %collective-permute-start.24 = (f32[256,256]{0,1:T(8,128)S(1)}, f32[256,256]{0,1:T(8,128)S(1)}, u32[]{:S(2)}, u32[]{:S(2)}) collective-permute-start(f32[256,256]{0,1:T(8,128)S(1)} %add.186), channel_id=1, source_target_pairs={{0,16},{4,20},{8,24},{12,28},{16,0},{20,4},{24,8},{28,12},{32,48},... | collective-permute-start | bytes 786440 | tf_op jit(solution)/shard_map/ppermute | solution.py:10
  398.6 6.5 %collective-permute-start.25 = (f32[256,256]{0,1:T(8,128)S(1)}, f32[256,256]{0,1:T(8,128)S(1)}, u32[]{:S(2)}, u32[]{:S(2)}) collective-permute-start(f32[256,256]{0,1:T(8,128)S(1)} %add.187), channel_id=1, source_target_pairs={{0,32},{4,36},{8,40},{12,44},{16,48},{20,52},{24,56},{28,60},{32,0... | collective-permute-start | bytes 786440 | tf_op jit(solution)/shard_map/ppermute | solution.py:10
  405.1 17.4 %copy-start.2 = (f32[2048,256]{1,0:T(8,128)S(1)}, f32[2048,256]{1,0:T(8,128)}, u32[]{:S(2)}) copy-start(f32[2048,256]{1,0:T(8,128)} %copy-done.1) | copy-start | bytes 6291460
  405.1 17.4 %copy-start.4 = (f32[2048,256]{1,0:T(8,128)S(1)}, f32[2048,256]{1,0:T(8,128)}, u32[]{:S(2)}) copy-start(f32[2048,256]{1,0:T(8,128)} %copy-done.3) | copy-start | bytes 6291460
  405.1 11.5 %collective-permute-start.26 = (f32[256,256]{0,1:T(8,128)S(1)}, f32[256,256]{0,1:T(8,128)S(1)}, u32[]{:S(2)}, u32[]{:S(2)}) collective-permute-start(f32[256,256]{0,1:T(8,128)S(1)} %add.188), channel_id=1, source_target_pairs={{0,64},{4,68},{8,72},{12,76},{16,80},{20,84},{24,88},{28,92},{32,9... | collective-permute-start | bytes 786440 | tf_op jit(solution)/shard_map/ppermute | solution.py:10
  416.7 16.5 %collective-permute-start.27 = (f32[256,256]{0,1:T(8,128)S(1)}, f32[256,256]{0,1:T(8,128)S(1)}, u32[]{:S(2)}, u32[]{:S(2)}) collective-permute-start(f32[256,256]{0,1:T(8,128)S(1)} %add.189), channel_id=1, source_target_pairs={{0,128},{4,132},{8,136},{12,140},{16,144},{20,148},{24,152},{28,15... | collective-permute-start | bytes 786440 | tf_op jit(solution)/shard_map/ppermute | solution.py:10
Sparse Core Ops, SparseCore 0:
  17.7 26.1 all-gather.12
  46.3 22.7 all-gather.14
  101.2 20.9 all-gather.16
  174.3 22.0 all-gather.18
  198.1 25.3 all-gather.20
  351.1 21.3 all-gather.22
